TPU v7x, 128 devices: a whole 4x4x4 slice. The times are simulated.
128 devices in a mesh: row: 8 (over y, core), col: 16 (over z, x).
Axes of the slice: x: 4, y: 4, z: 4, core: 2. Of those that a mesh axis runs over, the one named last changes fastest.
Arguments:
- amplitudes: bfloat16 [16, 16, 4, 128, 128], P('row', 'col'), may hold values from -6 to 6
- cholesky: bfloat16 [16, 16, 10, 128, 128], P('row', 'col'), may hold values from -0.5 to 0.5, as said below
- tile_mask: int32 [16, 16], P('row', 'col'), may hold values 0 or 1
Outputs:
- antisymmetrized: bfloat16 [16, 16, 4, 128, 128], P('row', 'col')
Inputs may be any that keep to these rules, and one draw needn't show every extreme that they name: cholesky is symmetric: cholesky[a,c,q,x,u] equals cholesky[c,a,q,u,x].
All inputs are finite; a program needn't handle non-finite values. No bound on the sum of `tile_mask` on one device may be relied on, other than what follows from the above.
Results may differ from a plain program's by a relative error of at most 0.0059.
Values may be sent and summed in bfloat16 or wider, within the bound.
A program may use at most 128 MiB of HBM per device.

v0:
```python
import math

import jax
import jax.numpy as jnp
from jax import lax
from jax.sharding import PartitionSpec as P


def from_partner(value, axis, apart):
    mask = 2**apart
    pairs = [(source, source ^ mask) for source in range(lax.axis_size(axis))]
    return lax.ppermute(value, axis, pairs)


def flip_row(tile_set, bit_pos):
    bit_value = lax.axis_index("row") >> bit_pos & 1
    kept = lax.dynamic_index_in_dim(tile_set, bit_value, 0, keepdims=False)
    outgoing = lax.dynamic_index_in_dim(tile_set, 1 - bit_value, 0, keepdims=False)
    incoming = from_partner(outgoing, "row", bit_pos)
    slot_zero = jnp.where(bit_value == 0, kept, incoming)
    slot_one = jnp.where(bit_value == 0, incoming, kept)
    return jnp.stack([slot_zero, slot_one])


def flip_col(tile_set, bit_pos):
    bit_value = lax.axis_index("col") >> bit_pos & 1
    kept = lax.dynamic_index_in_dim(tile_set, bit_value, 0, keepdims=False)
    outgoing = lax.dynamic_index_in_dim(tile_set, 1 - bit_value, 0, keepdims=False)
    incoming = from_partner(outgoing, "col", bit_pos)
    slot_zero = jnp.where(bit_value == 0, kept, incoming)
    slot_one = jnp.where(bit_value == 0, incoming, kept)
    return jnp.stack([slot_zero, slot_one])


def mirror_cascade(tile_set):
    col_bits = lax.axis_size("col").bit_length() - 1
    tile_set = flip_col(tile_set, 0)
    for bit_pos in range(1, col_bits):
        tile_set = flip_row(tile_set, bit_pos - 1)
        tile_set = flip_col(tile_set, bit_pos)
        tile_set = flip_row(tile_set, bit_pos - 1)
    return tile_set


def body(amplitudes, cholesky, tile_mask):
    tile_rows = amplitudes.shape[0]
    pair_count = amplitudes.shape[2]
    tile_edge = amplitudes.shape[3]
    vectors = cholesky.shape[2]
    occupied = math.isqrt(pair_count)
    column = lax.all_gather(cholesky, "row", axis=0, tiled=True)
    column_mats = jnp.transpose(column[:, 0], (0, 2, 1, 3)).reshape(
        column.shape[0], tile_edge, vectors * tile_edge
    )
    amp_block = lax.all_gather(amplitudes, "col", axis=1, tiled=True)
    mask_block = lax.all_gather(tile_mask, "col", axis=1, tiled=True)
    tile_count = amp_block.shape[1]
    masked = amp_block * mask_block.astype(jnp.bfloat16)[:, :, None, None, None]
    masked = masked.reshape(amp_block.shape[0], tile_count, pair_count * tile_edge, tile_edge)
    halves = jnp.einsum("cnmv,nvz->cmz", masked, column_mats, preferred_element_type=jnp.float32)
    halves = halves.astype(jnp.bfloat16).reshape(
        tile_rows, pair_count, tile_edge, vectors, tile_edge
    )
    spread = lax.all_gather(cholesky, "col", axis=1, tiled=True)
    ladder = lax.psum_scatter(
        jnp.einsum("caqux,cpuqy->apxy", spread, halves, preferred_element_type=jnp.float32),
        "row",
        scatter_dimension=0,
        tiled=True,
    )
    rounded = ladder.astype(jnp.bfloat16)
    mirror = mirror_cascade(rounded)
    own_tiles = lax.optimization_barrier(rounded).astype(jnp.float32)
    flipped = mirror.reshape(tile_rows, occupied, occupied, tile_edge, tile_edge)
    flipped = jnp.transpose(flipped, (0, 2, 1, 4, 3)).reshape(
        tile_rows, pair_count, tile_edge, tile_edge
    )
    result_tiles = (own_tiles - flipped.astype(jnp.float32)).astype(jnp.bfloat16)
    return result_tiles.reshape(tile_rows, 1, pair_count, tile_edge, tile_edge)


def solution(mesh):
    in_specs = (
        P("row", "col", None, None, None),
        P("row", "col", None, None, None),
        P("row", "col"),
    )
    out_specs = P("row", "col", None, None, None)
    return jax.shard_map(body, mesh=mesh, in_specs=in_specs, out_specs=out_specs, check_vma=False)
```

profile of v0, /device:TPU:24, one launch (start us, length us, event | category | flops | bytes accessed | tf_op | source)
XLA Modules:
  0.0 310.3 jit_solution(16139904179975113621)
XLA Ops:
  6.5 0.7 all-gather.5.cloned.1.call-update
  7.3 0.7 all-gather.7.cloned.1.call-update
  8.1 0.7 all-gather.9.cloned.1.call-update
  8.7 21.9 %all-gather = s32[16,1,2]{2,1,0:T(1,128)S(1)} all-gather(s32[1,1,2]{2,1,0:T(1,128)} %bitcast.173), channel_id=1, replica_groups=mesh['row'=8,'col'=16] {'col'}, dimensions={0}, use_global_device_ids=true | all-gather | bytes 136 | tf_op jit(solution)/shard_map/all_gather | solution.py:56
  30.6 0.1 copy.35
  30.7 1.2 dynamic-slice
  32.6 30.8 %all-gather.5.cloned.1.call-done = bf16[2,16,4,128,128]{4,3,2,1,0:T(8,128)(2,1)} async-done(((bf16[2,1,4,128,128]{4,3,2,1,0:T(8,128)(2,1)}), bf16[2,16,4,128,128]{4,3,2,1,0:T(8,128)(2,1)}) %all-gather.5.cloned.1.call-update) | async-done | bytes 4194320 | tf_op jit(solution)/shard_map/all_gather | solution.py:55
  63.4 4.6 %broadcast_multiply_fusion = bf16[2,16,4,128,128]{4,3,2,1,0:T(8,128)(2,1)} fusion(bf16[2,16,4,128,128]{4,3,2,1,0:T(8,128)(2,1)} %all-gather.5.cloned.1.call-done, bf16[2,16]{1,0:T(2,128)(2,1)S(1)} %convert_bitcast_fusion.1), kind=kLoop, calls=%fused_computation.5 | loop fusion | flops 2097152 | bytes 8388672 | tf_op jit(solution)/shard_map/mul | solution.py:58
  67.9 31.4 %all-gather.7.cloned.1.call-done = bf16[16,1,10,128,128]{4,3,2,1,0:T(8,128)(2,1)} async-done(((bf16[2,1,10,128,128]{4,3,2,1,0:T(8,128)(2,1)}), bf16[16,1,10,128,128]{4,3,2,1,0:T(8,128)(2,1)}) %all-gather.7.cloned.1.call-update) | async-done | bytes 5242896 | tf_op jit(solution)/shard_map/all_gather | solution.py:51
  99.3 7.8 %copy.36 = bf16[16,1,10,128,128]{3,4,2,0,1:T(8,128)(2,1)} copy(bf16[16,1,10,128,128]{4,3,2,1,0:T(8,128)(2,1)} %all-gather.7.cloned.1.call-done) | data formatting | bytes 10485760 | tf_op jit(solution)/shard_map/all_gather | solution.py:51
  107.1 9.0 %bitcast_convert_fusion = bf16[2,512,1280]{2,1,0:T(8,128)(2,1)S(1)} fusion(bf16[2,16,512,128]{3,2,1,0:T(8,128)(2,1)} %bitcast.167, bf16[16,128,1280,1]{1,2,0,3:T(8,128)(2,1)} %bitcast.166), kind=kOutput, calls=%fused_computation.2 | convolution fusion | flops 5370019840 | bytes 12058624 | tf_op jit(solution)/shard_map/cnmv,nvz->cmz/dot_general | solution.py:60
  116.1 3.2 %reshape.36 = bf16[2,4,128,10,128]{4,3,2,1,0:T(8,128)(2,1)} reshape(bf16[2,512,1280]{2,1,0:T(8,128)(2,1)S(1)} %bitcast_convert_fusion) | data formatting | bytes 5242880 | tf_op jit(solution)/shard_map/reshape | solution.py:61
  119.3 64.7 %all-gather.9.cloned.1.call-done = bf16[2,16,10,128,128]{4,3,2,0,1:T(8,128)(2,1)} async-done(((bf16[2,1,10,128,128]{4,3,2,0,1:T(8,128)(2,1)}), bf16[2,16,10,128,128]{4,3,2,0,1:T(8,128)(2,1)}) %all-gather.9.cloned.1.call-update) | async-done | bytes 10485776 | tf_op jit(solution)/shard_map/all_gather | solution.py:64
  183.9 10.9 %fusion.3 = f32[16,4,128,128]{2,3,0,1:T(8,128)} fusion(bf16[2,16,10,128,128]{4,3,2,0,1:T(8,128)(2,1)} %all-gather.9.cloned.1.call-done, bf16[2,4,128,10,128,1]{4,3,2,1,0,5:T(8,128)(2,1)} %bitcast.168), kind=kOutput, calls=%fused_computation.4 | convolution fusion | flops 5368709120 | bytes 17301504 | tf_op jit(solution)/shard_map/caqux,cpuqy->apxy/dot_general | solution.py:66
  194.8 55.0 %all-reduce.2 = bf16[16,4,128,128]{2,3,0,1:T(8,128)(2,1)S(1)} all-reduce(f32[16,4,128,128]{2,3,0,1:T(8,128)} %fusion.3), channel_id=2, replica_groups=mesh['row'=8,'col'=16] {'row'}, use_global_device_ids=true, to_apply=%region_0.0.clone | all-reduce | flops 1048576 | bytes 6291456
  249.8 0.2 copy.41
  250.0 1.5 collective-permute-start
  251.5 3.8 %collective-permute-done = bf16[4,128,128]{2,1,0:T(8,128)(2,1)S(1)} collective-permute-done((bf16[4,128,128]{2,1,0:T(8,128)(2,1)S(1)}, bf16[4,128,128]{2,1,0:T(8,128)(2,1)S(1)}, u32[]{:S(2)}, u32[]{:S(2)}) %collective-permute-start) | collective-permute-done | bytes 131104 | tf_op jit(solution)/shard_map/ppermute | solution.py:12
  255.4 0.1 fusion.42
  255.5 1.0 collective-permute-start.1
  256.5 1.0 collective-permute-done.1
  257.5 0.1 fusion.38
  257.6 3.0 collective-permute-start.2
  260.6 4.3 %collective-permute-done.2 = bf16[4,128,128]{2,1,0:T(8,128)(2,1)S(1)} collective-permute-done((bf16[4,128,128]{2,1,0:T(8,128)(2,1)S(1)}, bf16[4,128,128]{2,1,0:T(8,128)(2,1)S(1)}, u32[]{:S(2)}, u32[]{:S(2)}) %collective-permute-start.2) | collective-permute-done | bytes 131104 | tf_op jit(solution)/shard_map/ppermute | solution.py:12
  265.0 0.1 fusion.34
  265.1 0.1 collective-permute-start.3
  265.2 1.3 collective-permute-done.3
  266.6 0.1 fusion.30
  266.7 0.1 collective-permute-start.4
  266.8 5.5 %collective-permute-done.4 = bf16[4,128,128]{2,1,0:T(8,128)(2,1)S(1)} collective-permute-done((bf16[4,128,128]{2,1,0:T(8,128)(2,1)S(1)}, bf16[4,128,128]{2,1,0:T(8,128)(2,1)S(1)}, u32[]{:S(2)}, u32[]{:S(2)}) %collective-permute-start.4) | collective-permute-done | bytes 131104 | tf_op jit(solution)/shard_map/ppermute | solution.py:12
  272.4 0.1 fusion.26
  272.4 1.4 collective-permute-start.5
  273.8 3.7 %collective-permute-done.5 = bf16[4,128,128]{2,1,0:T(8,128)(2,1)S(1)} collective-permute-done((bf16[4,128,128]{2,1,0:T(8,128)(2,1)S(1)}, bf16[4,128,128]{2,1,0:T(8,128)(2,1)S(1)}, u32[]{:S(2)}, u32[]{:S(2)}) %collective-permute-start.5) | collective-permute-done | bytes 131104 | tf_op jit(solution)/shard_map/ppermute | solution.py:12
  277.5 0.1 fusion.22
  277.6 0.4 collective-permute-start.6
  278.1 4.6 %collective-permute-done.6 = bf16[4,128,128]{2,1,0:T(8,128)(2,1)S(1)} collective-permute-done((bf16[4,128,128]{2,1,0:T(8,128)(2,1)S(1)}, bf16[4,128,128]{2,1,0:T(8,128)(2,1)S(1)}, u32[]{:S(2)}, u32[]{:S(2)}) %collective-permute-start.6) | collective-permute-done | bytes 131104 | tf_op jit(solution)/shard_map/ppermute | solution.py:12
  282.7 0.1 fusion.18
  282.8 3.1 collective-permute-start.7
  285.9 3.5 %collective-permute-done.7 = bf16[4,128,128]{2,1,0:T(8,128)(2,1)S(1)} collective-permute-done((bf16[4,128,128]{2,1,0:T(8,128)(2,1)S(1)}, bf16[4,128,128]{2,1,0:T(8,128)(2,1)S(1)}, u32[]{:S(2)}, u32[]{:S(2)}) %collective-permute-start.7) | collective-permute-done | bytes 131104 | tf_op jit(solution)/shard_map/ppermute | solution.py:12
  289.4 0.1 fusion.14
  289.5 3.0 collective-permute-start.8
  292.5 3.6 %collective-permute-done.8 = bf16[4,128,128]{2,1,0:T(8,128)(2,1)S(1)} collective-permute-done((bf16[4,128,128]{2,1,0:T(8,128)(2,1)S(1)}, bf16[4,128,128]{2,1,0:T(8,128)(2,1)S(1)}, u32[]{:S(2)}, u32[]{:S(2)}) %collective-permute-start.8) | collective-permute-done | bytes 131104 | tf_op jit(solution)/shard_map/ppermute | solution.py:12
  296.1 0.1 fusion.10
  296.2 3.1 collective-permute-start.9
  299.3 3.5 %collective-permute-done.9 = bf16[4,128,128]{2,1,0:T(8,128)(2,1)S(1)} collective-permute-done((bf16[4,128,128]{2,1,0:T(8,128)(2,1)S(1)}, bf16[4,128,128]{2,1,0:T(8,128)(2,1)S(1)}, u32[]{:S(2)}, u32[]{:S(2)}) %collective-permute-start.9) | collective-permute-done | bytes 131104 | tf_op jit(solution)/shard_map/ppermute | solution.py:12
  302.7 0.1 broadcast_select_fusion.1
  302.9 0.2 copy.42
  303.1 0.8 fusion.8
  (16 shorter events, 0.7 us)
Async XLA Ops:
  6.5 56.8 %all-gather.5.cloned.1.call-start = ((), (), s32[]{:S(2)}) async-start(), calls=%async_computation | async-start | bytes 4456448 | tf_op jit(solution)/shard_map/all_gather | solution.py:55
  7.3 92.0 %all-gather.7.cloned.1.call-start = ((), (), s32[]{:S(2)}) async-start(), calls=%async_computation.1 | async-start | bytes 5898240 | tf_op jit(solution)/shard_map/all_gather | solution.py:51
  8.0 175.9 %all-gather.9.cloned.1.call-start = ((), (), s32[]{:S(2)}) async-start(), calls=%async_computation.2 | async-start | bytes 11141120 | tf_op jit(solution)/shard_map/all_gather | solution.py:64
  250.0 5.3 %collective-permute-start = (bf16[4,128,128]{2,1,0:T(8,128)(2,1)S(1)}, bf16[4,128,128]{2,1,0:T(8,128)(2,1)S(1)}, u32[]{:S(2)}, u32[]{:S(2)}) collective-permute-start(bf16[4,128,128]{2,1,0:T(8,128)(2,1)S(1)} %dynamic-slice_bitcast_fusion), channel_id=1, source_target_pairs={{0,1},{1,0},{2,3},{3,2},{4,5},{5,4},{6,7},{7,6},{8,9},{9,8},{10,11... | collective-permute-start | bytes 393224 | tf_op jit(solution)/shard_map/ppermute | solution.py:12
  255.5 2.0 collective-permute-start.1
  257.6 7.3 %collective-permute-start.2 = (bf16[4,128,128]{2,1,0:T(8,128)(2,1)S(1)}, bf16[4,128,128]{2,1,0:T(8,128)(2,1)S(1)}, u32[]{:S(2)}, u32[]{:S(2)}) collective-permute-start(bf16[4,128,128]{2,1,0:T(8,128)(2,1)S(1)} %fusion.38), channel_id=1, source_target_pairs={{0,2},{1,3},{2,0},{3,1},{4,6},{5,7},{6,4},{7,5},{8,10},{9,11},{10,... | collective-permute-start | bytes 393224 | tf_op jit(solution)/shard_map/ppermute | solution.py:12
  265.1 1.4 collective-permute-start.3
  266.7 5.6 %collective-permute-start.4 = (bf16[4,128,128]{2,1,0:T(8,128)(2,1)S(1)}, bf16[4,128,128]{2,1,0:T(8,128)(2,1)S(1)}, u32[]{:S(2)}, u32[]{:S(2)}) collective-permute-start(bf16[4,128,128]{2,1,0:T(8,128)(2,1)S(1)} %fusion.30), channel_id=1, source_target_pairs={{0,32},{16,48},{32,0},{48,16},{64,96},{80,112},{96,64},{112,80},{1... | collective-permute-start | bytes 393224 | tf_op jit(solution)/shard_map/ppermute | solution.py:12
  272.4 5.0 %collective-permute-start.5 = (bf16[4,128,128]{2,1,0:T(8,128)(2,1)S(1)}, bf16[4,128,128]{2,1,0:T(8,128)(2,1)S(1)}, u32[]{:S(2)}, u32[]{:S(2)}) collective-permute-start(bf16[4,128,128]{2,1,0:T(8,128)(2,1)S(1)} %fusion.26), channel_id=1, source_target_pairs={{0,4},{1,5},{2,6},{3,7},{4,0},{5,1},{6,2},{7,3},{8,12},{9,13},{10,... | collective-permute-start | bytes 393224 | tf_op jit(solution)/shard_map/ppermute | solution.py:12
  277.6 5.0 %collective-permute-start.6 = (bf16[4,128,128]{2,1,0:T(8,128)(2,1)S(1)}, bf16[4,128,128]{2,1,0:T(8,128)(2,1)S(1)}, u32[]{:S(2)}, u32[]{:S(2)}) collective-permute-start(bf16[4,128,128]{2,1,0:T(8,128)(2,1)S(1)} %fusion.22), channel_id=1, source_target_pairs={{0,32},{16,48},{32,0},{48,16},{64,96},{80,112},{96,64},{112,80},{1... | collective-permute-start | bytes 393224 | tf_op jit(solution)/shard_map/ppermute | solution.py:12
  282.8 6.6 %collective-permute-start.7 = (bf16[4,128,128]{2,1,0:T(8,128)(2,1)S(1)}, bf16[4,128,128]{2,1,0:T(8,128)(2,1)S(1)}, u32[]{:S(2)}, u32[]{:S(2)}) collective-permute-start(bf16[4,128,128]{2,1,0:T(8,128)(2,1)S(1)} %fusion.18), channel_id=1, source_target_pairs={{0,64},{16,80},{32,96},{48,112},{64,0},{80,16},{96,32},{112,48},{1... | collective-permute-start | bytes 393224 | tf_op jit(solution)/shard_map/ppermute | solution.py:12
  289.5 6.6 %collective-permute-start.8 = (bf16[4,128,128]{2,1,0:T(8,128)(2,1)S(1)}, bf16[4,128,128]{2,1,0:T(8,128)(2,1)S(1)}, u32[]{:S(2)}, u32[]{:S(2)}) collective-permute-start(bf16[4,128,128]{2,1,0:T(8,128)(2,1)S(1)} %fusion.14), channel_id=1, source_target_pairs={{0,8},{1,9},{2,10},{3,11},{4,12},{5,13},{6,14},{7,15},{8,0},{9,1},... | collective-permute-start | bytes 393224 | tf_op jit(solution)/shard_map/ppermute | solution.py:12
  296.2 6.6 %collective-permute-start.9 = (bf16[4,128,128]{2,1,0:T(8,128)(2,1)S(1)}, bf16[4,128,128]{2,1,0:T(8,128)(2,1)S(1)}, u32[]{:S(2)}, u32[]{:S(2)}) collective-permute-start(bf16[4,128,128]{2,1,0:T(8,128)(2,1)S(1)} %fusion.10), channel_id=1, source_target_pairs={{0,64},{16,80},{32,96},{48,112},{64,0},{80,16},{96,32},{112,48},{1... | collective-permute-start | bytes 393224 | tf_op jit(solution)/shard_map/ppermute | solution.py:12
Sparse Core Ops, SparseCore 0:
  9.5 53.8 all-gather.4
  65.1 34.1 all-gather.6
  101.4 82.4 all-gather.8
where the time goes:
time: 315 us; the launch traced here: 310 us
  waiting for transfers between devices  164 us (52%)
  blocking collectives  76.8 us (24%)
  matrix products  19.9 us (6%)
  starting transfers between devices  16.7 us (5%)
  between operations  14 us (4%)
  local copies, waits for them, and re-layouts  12.7 us (4%)
  other arithmetic  6.55 us (2%)
    all_gather x1, waiting for transfers between devices, body(): spread = lax.all_gather(cholesky, 'col', axis=1, tiled=True)  64.7 us
    unnamed x1, blocking collectives  55 us
    ppermute x10, waiting for transfers between devices, from_partner(): return lax.ppermute(value, axis, pairs)  34.8 us
    all_gather x1, waiting for transfers between devices, body(): column = lax.all_gather(cholesky, 'row', axis=0, tiled=True)  31.4 us
    all_gather x1, waiting for transfers between devices, body(): amp_block = lax.all_gather(amplitudes, 'col', axis=1, tiled=True)  30.8 us
    all_gather x1, blocking collectives, body(): mask_block = lax.all_gather(tile_mask, 'col', axis=1, tiled=True)  21.9 us
    ppermute x10, starting transfers between devices, from_partner(): return lax.ppermute(value, axis, pairs)  16.7 us
    dot_general x1, matrix products, body(): jnp.einsum('caqux,cpuqy->apxy', spread, halves, preferred_element_type=jn...  10.9 us
  transfers between devices with their start and end apart: 13, of which 13 were waited for; matrix products, arithmetic and copies ran while one was open for 8% of the time, Pallas kernels for 0%

commit v1 on v0

v1 whole, which is shorter than its diff:
```python
import jax
import jax.numpy as jnp
from jax import lax
from jax.experimental import pallas as pl
from jax.experimental.pallas import tpu as pltpu
from jax.sharding import PartitionSpec as P

MESH = pl.DeviceIdType.MESH
BF16 = jnp.bfloat16
F32 = jnp.float32
MAX_COPIES = 192
MAX_LOCAL = 64


def kernel(
    lin, t, out, zl, yl, ag, mt, g, ob, rz, rx, s0, s1, f0, f1, fo, mo, ssem, rsem, lsem
):
    r = lax.axis_index("row")
    col = lax.axis_index("col")
    y, k = lax.div(r, 2), lax.rem(r, 2)
    z, x = lax.div(col, 4), lax.rem(col, 4)

    def around(v):
        return lax.rem(v + 1, 4), lax.rem(v + 3, 4), lax.rem(v + 2, 4)

    xp, xm, x2 = around(x)
    yp, ym, y2 = around(y)
    zp, zm, z2 = around(z)

    def dev(x_=x, y_=y, z_=z, k_=k):
        return (2 * y_ + k_, 4 * z_ + x_)

    count = [0, 0]
    sent = []
    local = []

    def send(src, dst, to):
        i = count[0]
        count[0] += 1
        cp = pltpu.make_async_remote_copy(
            src_ref=src,
            dst_ref=dst,
            send_sem=ssem.at[i],
            recv_sem=rsem.at[i],
            device_id=to,
            device_id_type=MESH,
        )
        cp.start()
        sent.append(cp)
        return cp

    def copy(src, dst):
        i = count[1]
        count[1] += 1
        cp = pltpu.make_async_copy(src, dst, lsem.at[i])
        cp.start()
        return cp

    def exchange(src, dst):
        plans = []
        n = count[0]
        m = count[1]
        count[0] += 2
        count[1] += 2
        slot = lax.rem(x, 2)
        for i in range(2):
            x_to = 2 * k + i
            same = (y == z) & (x == x_to)
            to = dev(x_=x_to, y_=z, z_=y, k_=lax.div(x, 2))

            def remote(lands, i=i, to=to):
                return pltpu.make_async_remote_copy(
                    src_ref=src(i),
                    dst_ref=dst(lands),
                    send_sem=ssem.at[n + i],
                    recv_sem=rsem.at[n + lands],
                    device_id=to,
                    device_id_type=MESH,
                )

            here = pltpu.make_async_copy(src(i), dst(i), lsem.at[m + i])
            plans.append((same, remote(slot), remote(i), here))
        for same, there, back, here in plans:
            pl.when(jnp.logical_not(same))(there.start)
            pl.when(same)(here.start)
        return plans

    def exchange_wait(plans, i):
        same, there, back, here = plans[i]

        def both():
            there.wait_send()
            back.wait_recv()

        pl.when(jnp.logical_not(same))(both)
        pl.when(same)(here.wait)

    mine = copy(lin.at[:, pl.ds(2 * x, 2)], zl.at[z, :, x, pl.ds(0, 2)])
    mine_h = copy(lin.at[:, 8 + lax.div(x, 2)], zl.at[z, :, x, 2])
    mirrored = exchange(lambda i: t.at[i, pl.ds(1, 3)], lambda i: mt.at[i])
    spread = {}
    for off in (1, 3, 2):
        xt = lax.rem(x + off, 4)
        spread[off] = (
            send(lin.at[:, pl.ds(2 * xt, 2)], zl.at[z, :, x, pl.ds(0, 2)], dev(x_=xt)),
            send(lin.at[:, 8 + lax.div(xt, 2)], zl.at[z, :, x, 2], dev(x_=xt)),
        )
    mine.wait()
    mine_h.wait()

    chunk = [x, xm, xp, x2]
    offs = [0, 1, 3, 2]
    zc, yc = {}, {}
    rr = [r, 2 * ym + k, 2 * yp + k, 2 * y2 + k]
    partner = dev(k_=1 - k)
    locals_ = []

    def send_chunk(j):
        xs = chunk[j]
        src = zl.at[z, :, xs]
        zc[j] = [send(src, src, dev(z_=zp)), send(src, src, dev(z_=zm))]
        dst = yl.at[r, :, xs]
        yc[j] = [
            send(src, dst, dev(y_=yp)),
            send(src, dst, dev(y_=ym)),
            send(src, dst, partner),
        ]
        locals_.append(copy(src, dst))

    def forward_chunk(j):
        xs = chunk[j]
        zc[j][0].wait_recv()
        blk = zl.at[zm, 0, xs]
        zc[j].append(send(blk, blk, dev(z_=zp)))
        zc[j][1].wait_recv()
        blk = zl.at[zp, 1, xs]
        zc[j].append(send(blk, blk, dev(z_=zm)))
        yc[j][0].wait_recv()
        blk = yl.at[rr[1], 0, xs]
        yc[j].append(send(blk, blk, dev(y_=yp)))
        blk = yl.at[rr[1], :, xs]
        yc[j].append(send(blk, blk, partner))
        yc[j][1].wait_recv()
        blk = yl.at[rr[2], 1, xs]
        yc[j].append(send(blk, blk, dev(y_=ym)))
        blk = yl.at[rr[2], :, xs]
        yc[j].append(send(blk, blk, partner))

    def finish_chunk(j):
        xs = chunk[j]
        yc[j][3].wait_recv()
        yc[j][5].wait_recv()
        blk = yl.at[rr[3], :, xs]
        yc[j].append(send(blk, blk, partner))

    ac, pc = {}, []

    def send_a(b):
        blk = ag.at[rr[b], :, x]
        ac[b] = [
            send(blk, blk, dev(x_=xp)),
            send(blk, blk, dev(x_=xm)),
        ]
        pc.append(send(blk, blk, partner))

    def forward_a(b):
        ac[b][0].wait_recv()
        blk = ag.at[rr[b], 0, xm]
        ac[b].append(send(blk, blk, dev(x_=xp)))
        blk = ag.at[rr[b], :, xm]
        pc.append(send(blk, blk, partner))
        ac[b][1].wait_recv()
        blk = ag.at[rr[b], 1, xp]
        ac[b].append(send(blk, blk, dev(x_=xm)))
        blk = ag.at[rr[b], :, xp]
        pc.append(send(blk, blk, partner))

    def finish_a(b):
        ac[b][2].wait_recv()
        ac[b][3].wait_recv()
        blk = ag.at[rr[b], :, x2]
        pc.append(send(blk, blk, partner))

    send_chunk(0)

    for i in range(2):
        exchange_wait(mirrored, i)
    for i in range(2):
        for p, (own, other) in enumerate(((0, 1), (1, 0), (3, 2))):
            diff = t[i, own].astype(F32) - mt[i, other].astype(F32).T
            ag[r, i, x, p] = diff.astype(BF16)
    blk = ag.at[r, :, x]
    a_up = send(blk, blk, dev(y_=yp))
    a_dn = send(blk, blk, dev(y_=ym))
    send_a(0)

    def arrive(j):
        for cp in spread[offs[j]]:
            cp.wait_recv()
        send_chunk(j)

    arrive(1)
    arrive(2)
    forward_chunk(0)
    a_up.wait_recv()
    blk = ag.at[rr[1], 0, x]
    a_up2 = send(blk, blk, dev(y_=yp))
    send_a(1)
    a_dn.wait_recv()
    blk = ag.at[rr[2], 1, x]
    a_dn2 = send(blk, blk, dev(y_=ym))
    send_a(2)
    arrive(3)
    forward_chunk(1)
    forward_a(0)
    forward_chunk(2)
    a_up2.wait_recv()
    a_dn2.wait_recv()
    send_a(3)
    forward_a(1)
    forward_a(2)
    forward_chunk(3)
    forward_a(3)
    for j in range(4):
        finish_chunk(j)
    for b in range(4):
        finish_a(b)
    for j in range(4):
        zc[j][2].wait_recv()
        zc[j][3].wait_recv()
        for n in (2, 4, 6, 7):
            yc[j][n].wait_recv()
    for cp in pc:
        cp.wait_recv()
    for cp in locals_:
        cp.wait()

    half = 2 * lax.rem(x, 2)
    red = {}

    def lhs_of(q):
        rows = [
            jnp.concatenate(
                [zl[dz, i, dx, q] for dz in range(4) for dx in range(4)], axis=1
            )
            for i in range(2)
        ]
        return jnp.concatenate(rows, axis=0)

    for p in range(3):
        full = jnp.concatenate(
            [
                jnp.concatenate([ag[d // 2, d % 2, c, p] for c in range(4)], axis=1)
                for d in range(16)
            ],
            axis=0,
        )
        for q in range(2):
            g[p, :, q * 512 : (q + 1) * 512] = jnp.dot(
                lhs_of(q), full, preferred_element_type=F32
            ).astype(BF16)
        part = jnp.concatenate(
            [
                jnp.concatenate(
                    [ag[d // 2, d % 2, half + c, p] for c in range(2)], axis=1
                )
                for d in range(16)
            ],
            axis=0,
        )
        g[p, :, 1024:1280] = jnp.dot(
            lhs_of(2), part, preferred_element_type=F32
        ).astype(BF16)

        def tile_pair(a, carry, p=p):
            rows = []
            for i in range(2):
                tiles = [yl[a, i, c, q] for q in range(2) for c in range(4)]
                tiles += [yl[a, i, half + c, 2] for c in range(2)]
                rows.append(jnp.concatenate(tiles, axis=1))
            right = jnp.concatenate(rows, axis=0)
            res = lax.dot_general(
                g[p],
                right,
                (((1,), (1,)), ((), ())),
                preferred_element_type=F32,
            ).astype(BF16)
            az, ax = lax.div(a, 2), 2 * lax.rem(a, 2)
            for i in range(2):
                for n in range(2):
                    ob[p, i, az, ax + n] = res[
                        i * 128 : (i + 1) * 128, n * 128 : (n + 1) * 128
                    ]
            return carry

        lax.fori_loop(0, 8, tile_pair, 0)
        red[p] = []
        for off in (1, 3, 2):
            zt, xt = lax.rem(z + off, 4), lax.rem(x + off, 4)
            red[p].append(send(ob.at[p, 0, zt], rz.at[p, z], dev(z_=zt)))
            red[p].append(send(ob.at[p, 1, :, xt], rx.at[p, x], dev(x_=xt)))
        rz[p, z] = ob[p, 0, z]
        rx[p, x] = ob[p, 1, :, x]

    last = {}

    def total(ref, p):
        acc = ref[p, 0].astype(F32)
        for n in range(1, 4):
            acc = acc + ref[p, n].astype(F32)
        return acc.astype(BF16)

    for p in range(3):
        for cp in red[p]:
            cp.wait_recv()
        s0[p] = total(rz, p)
        s1[p] = total(rx, p)
        last[p] = []
        for off in (1, 3, 2):
            zt, xt = lax.rem(z + off, 4), lax.rem(x + off, 4)
            last[p].append(send(s0.at[p, xt], f0.at[p, x], dev(x_=xt)))
            last[p].append(send(s1.at[p, zt], f1.at[p, z], dev(z_=zt)))
        f0[p, x] = s0[p, x]
        f1[p, z] = s1[p, z]

    for p in range(3):
        for cp in last[p]:
            cp.wait_recv()
        to = (1, 0, 3)[p]
        tiles = (total(f0, p), total(f1, p))
        for i in range(2):
            out[i, 0, to] = tiles[i]
            if p == 0:
                fo[i] = tiles[i]
        if p == 0:
            swapped = exchange(lambda i: fo.at[i], lambda i: mo.at[i])
    for i in range(2):
        exchange_wait(swapped, i)
    for i in range(2):
        out[i, 0, 2] = (-mo[i].astype(F32).T).astype(BF16)
    for cp in sent:
        cp.wait_send()


def body(amplitudes, cholesky, tile_mask):
    keep = (tile_mask != 0)[:, :, None, None]
    amp = amplitudes[:, 0]
    order = jnp.stack([amp[:, p] for p in (1, 0, 2, 3)], axis=1)
    masked = jnp.where(keep, order, jnp.zeros_like(order))
    vec = cholesky[:, 0]
    vmem = pl.BlockSpec(memory_space=pltpu.VMEM)
    tile = (128, 128)
    return pl.pallas_call(
        kernel,
        out_shape=jax.ShapeDtypeStruct((2, 1, 4) + tile, BF16),
        in_specs=[vmem, vmem],
        out_specs=vmem,
        scratch_shapes=[
            pltpu.VMEM((4, 2, 4, 3) + tile, BF16),
            pltpu.VMEM((8, 2, 4, 3) + tile, BF16),
            pltpu.VMEM((8, 2, 4, 3) + tile, BF16),
            pltpu.VMEM((2, 3) + tile, BF16),
            pltpu.VMEM((3, 256, 1280), BF16),
            pltpu.VMEM((3, 2, 4, 4) + tile, BF16),
            pltpu.VMEM((3, 4, 4) + tile, BF16),
            pltpu.VMEM((3, 4, 4) + tile, BF16),
            pltpu.VMEM((3, 4) + tile, BF16),
            pltpu.VMEM((3, 4) + tile, BF16),
            pltpu.VMEM((3, 4) + tile, BF16),
            pltpu.VMEM((3, 4) + tile, BF16),
            pltpu.VMEM((2,) + tile, BF16),
            pltpu.VMEM((2,) + tile, BF16),
            pltpu.SemaphoreType.DMA((MAX_COPIES,)),
            pltpu.SemaphoreType.DMA((MAX_COPIES,)),
            pltpu.SemaphoreType.DMA((MAX_LOCAL,)),
        ],
        compiler_params=pltpu.CompilerParams(
            has_side_effects=True, vmem_limit_bytes=56 * 1024 * 1024
        ),
    )(vec, masked)


def solution(mesh):
    in_specs = (
        P("row", "col", None, None, None),
        P("row", "col", None, None, None),
        P("row", "col"),
    )
    out_specs = P("row", "col", None, None, None)
    return jax.shard_map(
        body, mesh=mesh, in_specs=in_specs, out_specs=out_specs, check_vma=False
    )
```

time: 315 us -> 99.4 us (0.32); the launches traced: 310 us -> 99.2 us
  waiting for transfers between devices: 164 us -> 0 us
  Pallas kernels: 0 us -> 95.1 us
  blocking collectives: 76.8 us -> 0 us
  matrix products: 19.9 us -> 0 us
  starting transfers between devices: 16.7 us -> 0 us
  between operations: 14 us -> 0.03 us
  local copies, waits for them, and re-layouts: 12.7 us -> 2.6 us
  other arithmetic: 6.55 us -> 1.5 us
    all_gather x3 -> x0, waiting for transfers between devices: 127 us -> none  [the longest x1 64.7 us: body(): spread = lax.all_gather(cholesky, 'col', axis=1, tiled=True)]
    pallas_call x0 -> x1, Pallas kernels: none -> 95.1 us  [body(): pl.pallas_call(kernel, out_shape=jax.ShapeDtypeStruct((2, 1, 4) + tile, B...]
    unnamed x1 -> x0, blocking collectives: 55 us -> none
    ppermute x10 -> x0, waiting for transfers between devices: 34.8 us -> none  [from_partner(): return lax.ppermute(value, axis, pairs)]
    all_gather x1 -> x0, blocking collectives: 21.9 us -> none  [body(): mask_block = lax.all_gather(tile_mask, 'col', axis=1, tiled=True)]
    dot_general x2 -> x0, matrix products: 19.9 us -> none  [the longest x1 10.9 us: body(): jnp.einsum('caqux,cpuqy->apxy', spread, halves, preferred_element_type=jn...]
    ppermute x10 -> x0, starting transfers between devices: 16.7 us -> none  [from_partner(): return lax.ppermute(value, axis, pairs)]
    all_gather x2 -> x0, local copies, waits for them, and re-layouts: 7.87 us -> none  [the longest x1 7.8 us: body(): column = lax.all_gather(cholesky, 'row', axis=0, tiled=True)]
  transfers between devices with their start and end apart: 13 -> 0, of which waited for: 13 -> 0; matrix products, arithmetic and copies ran while one was open for 8% -> 0% of each run, Pallas kernels for 0% -> 0%
where the time goes in v1:
time: 99.4 us; the launch traced here: 99.2 us
  Pallas kernels  95.1 us (96%)
  local copies, waits for them, and re-layouts  2.6 us (3%)
  other arithmetic  1.5 us (2%)
    pallas_call x1, Pallas kernels, body(): pl.pallas_call(kernel, out_shape=jax.ShapeDtypeStruct((2, 1, 4) + tile, B...  95.1 us

profile of v1, /device:TPU:24, one launch (start us, length us, event | category | flops | bytes accessed | tf_op | source)
XLA Modules:
  0.0 99.2 jit_solution(13199343984331158233)
XLA Ops:
  0.0 0.0 copy-start
  0.0 0.7 compare_bitcast_fusion
  0.7 0.9 slice.16
  1.6 0.0 copy-done
  1.7 0.8 maximum_select_fusion.t
  2.4 95.1 %shard_map.37 = bf16[2,1,4,128,128]{4,3,2,1,0:T(8,128)(2,1)} custom-call(bf16[2,10,128,128]{3,2,1,0:T(8,128)(2,1)} %bitcast.4, bf16[2,4,128,128]{3,2,1,0:T(8,128)(2,1)} %maximum_select_fusion.t), custom_call_target="tpu_custom_call" | custom-call | tf_op jit(solution)/shard_map/pallas_call | solution.py:353
  97.5 1.7 %copy.5 = bf16[2,1,4,128,128]{4,3,2,1,0:T(8,128)(2,1)} copy(bf16[2,1,4,128,128]{4,3,2,1,0:T(8,128)(2,1)} %shard_map.37) | data formatting | bytes 524288
  (1 shorter events, 0.0 us)
Async XLA Ops:
  0.0 1.6 %copy-start = (bf16[2,1,4,128,128]{4,3,2,1,0:T(8,128)(2,1)S(1)}, bf16[2,1,4,128,128]{4,3,2,1,0:T(8,128)(2,1)}, u32[]{:S(2)}) copy-start(bf16[2,1,4,128,128]{4,3,2,1,0:T(8,128)(2,1)} %param.3) | copy-start | bytes 786436

commit v2 on v0

v2 whole, which is shorter than its diff:
```python
import math

import jax
import jax.numpy as jnp
from jax import lax
from jax.experimental import pallas as pl
from jax.experimental.pallas import tpu as pltpu
from jax.sharding import PartitionSpec as P

MESH = pl.DeviceIdType.MESH
BF16 = jnp.bfloat16
F32 = jnp.float32
SENDS = 6
RECVS = 110
LOCALS = 16


def kernel(
    mask, lin, t_in, out, t, zl, yl, ag, mt, g, ob, rz, rx, s0, s1, f0, f1, fo, mo,
    size, ssem, rsem, lsem, xsem,
):
    r = lax.axis_index("row")
    col = lax.axis_index("col")
    y, k = lax.div(r, 2), lax.rem(r, 2)
    z, x = lax.div(col, 4), lax.rem(col, 4)

    def ring(v):
        return v, lax.rem(v + 3, 4), lax.rem(v + 1, 4), lax.rem(v + 2, 4)

    xs, ys, zs = ring(x), ring(y), ring(z)

    def dev(x_=x, y_=y, z_=z, k_=k):
        return (2 * y_ + k_, 4 * z_ + x_)

    to_x = [dev(x_=v) for v in xs]
    to_y = [dev(y_=v) for v in ys]
    to_z = [dev(z_=v) for v in zs]
    partner = dev(k_=1 - k)

    used = {"recv": 0, "local": 0, "swap": 0}
    load = [0] * SENDS

    def arrival():
        used["recv"] += 1
        return [rsem.at[used["recv"] - 1], 0]

    def await_tiles(due):
        blk = size.at[pl.ds(0, due[1])]
        pltpu.make_async_copy(blk, blk, due[0]).wait()

    def send(src, dst, to, group, due=None):
        due = due or arrival()
        tiles = math.prod(src.shape) // (128 * 128)
        due[1] += tiles
        load[group] += tiles
        pltpu.make_async_remote_copy(
            src_ref=src,
            dst_ref=dst,
            send_sem=ssem.at[group],
            recv_sem=due[0],
            device_id=to,
            device_id_type=MESH,
        ).start()
        return due

    def copy(src, dst):
        cp = pltpu.make_async_copy(src, dst, lsem.at[used["local"]])
        used["local"] += 1
        cp.start()
        return cp

    def mirror_of(i):
        return (y == z) & (x == 2 * k + i), dev(
            x_=2 * k + i, y_=z, z_=y, k_=lax.div(x, 2)
        )

    def exchange(src, dst):
        plans = []
        n = used["swap"]
        used["swap"] += 6
        slot = lax.rem(x, 2)
        for i in range(2):
            same, to = mirror_of(i)

            def remote(lands, i=i, to=to):
                return pltpu.make_async_remote_copy(
                    src_ref=src(i),
                    dst_ref=dst(lands),
                    send_sem=xsem.at[n + i],
                    recv_sem=xsem.at[n + 2 + lands],
                    device_id=to,
                    device_id_type=MESH,
                )

            here = pltpu.make_async_copy(src(i), dst(i), xsem.at[n + 4 + i])
            plans.append((same, remote(slot), remote(i), here))
        for same, there, back, here in plans:
            pl.when(jnp.logical_not(same))(there.start)
            pl.when(same)(here.start)
        return plans

    def exchange_wait(plans):
        for same, there, back, here in plans:

            def both(there=there, back=back):
                there.wait_send()
                back.wait_recv()

            pl.when(jnp.logical_not(same))(both)
            pl.when(same)(here.wait)

    barrier = pltpu.get_barrier_semaphore()

    def greet(to):
        pl.semaphore_signal(barrier, inc=1, device_id=to, device_id_type=MESH)

    selfs = jnp.int32(0)
    for i in range(2):
        same, to = mirror_of(i)
        selfs = selfs + jnp.where(same, 1, 0)
        pl.when(jnp.logical_not(same))(lambda to=to: greet(to))
    near = to_z[1:] + to_x[1:] + to_y[1:3] + [partner]
    for to in near:
        greet(to)
    mine = copy(lin.at[:, pl.ds(2 * x, 2)], zl.at[z, :, x, pl.ds(0, 2)])
    mine_h = copy(lin.at[:, 8 + lax.div(x, 2)], zl.at[z, :, x, 2])
    for i in range(2):
        flag = mask[0, i].astype(F32)
        for p in range(4):
            tile = (t_in[i, 0, p].astype(F32) * flag).astype(BF16)
            if p:
                t[i, p - 1] = tile
            else:
                ag[0, y, k, i, x] = tile
    mine.wait()
    mine_h.wait()
    pl.semaphore_wait(barrier, len(near) + 2 - selfs)

    class Gather:
        def __init__(self, p, y_first):
            self.p = p
            self.y_first = y_first
            self.one, self.two = (to_y, to_x) if y_first else (to_x, to_y)
            self.near = [None] * 4
            self.far = arrival()
            self.other = arrival()

        def block(self, n, m, rows=slice(None)):
            a, b = (n, m) if self.y_first else (m, n)
            return ag.at[self.p, ys[a], k, rows, xs[b]]

        def spread_second(self, n):
            blk = self.block(n, 0)
            self.near[n] = [
                send(blk, blk, self.two[2], 3),
                send(blk, blk, self.two[1], 3),
            ]

        def start(self):
            blk = self.block(0, 0)
            self.first = [send(blk, blk, self.one[2], 3), send(blk, blk, self.one[1], 3)]
            self.first.append(arrival())

        def middle(self):
            for n, row, m in ((1, 0, 2), (2, 1, 1)):
                await_tiles(self.first[n - 1])
                blk = self.block(n, 0, row)
                send(blk, blk, self.one[m], 3, self.first[2])
                self.spread_second(n)

        def across(self):
            await_tiles(self.first[2])
            self.spread_second(3)
            self.hand_over(0)

        def forward(self, n):
            for b, row, m in ((1, 0, 2), (2, 1, 1)):
                await_tiles(self.near[n][b - 1])
                blk = self.block(n, b, row)
                send(blk, blk, self.two[m], 3, self.far)

        def hand_over(self, m):
            if self.y_first:
                blk = ag.at[self.p, :, k, :, xs[m]]
            else:
                blk = ag.at[self.p, ys[m], k]
            send(blk, blk, partner, 4, self.other)

        def hand_near(self):
            self.hand_over(1)
            self.hand_over(2)

        def hand_far(self):
            await_tiles(self.far)
            self.hand_over(3)

        def done(self):
            await_tiles(self.other)

    a0, a1, a2 = (Gather(p, True) for p in range(3))

    a0.start()
    swaps = [
        exchange(lambda i, q=q: t.at[i, q], lambda i, q=q: mt.at[q - 1, i])
        for q in (1, 2)
    ]

    def form(p):
        own, other = ((0, 0), (2, 1))[p - 1]
        exchange_wait(swaps[p - 1])
        for i in range(2):
            diff = t[i, own].astype(F32) - mt[other, i].astype(F32).T
            ag[p, y, k, i, x] = diff.astype(BF16)

    spread = [None] * 4
    for n, m in ((1, 2), (2, 1), (3, 3)):
        v = xs[m]
        spread[n] = arrival()
        src = lin.at[:, pl.ds(2 * v, 2)]
        send(src, zl.at[z, :, x, pl.ds(0, 2)], to_x[m], 0, spread[n])
        src = lin.at[:, 8 + lax.div(v, 2)]
        send(src, zl.at[z, :, x, 2], to_x[m], 0, spread[n])

    zc, yc, yp = [None] * 4, [None] * 4, [None] * 4
    depth = (3, 2, 2, 3)
    own_copies = []

    def z_send(j):
        src = zl.at[z, :, xs[j]]
        zc[j] = [send(src, src, to_z[2], 0), send(src, src, to_z[1], 0), arrival()]

    def z_forward(j):
        for n, row, m in ((1, 0, 2), (2, 1, 1)):
            await_tiles(zc[j][n - 1])
            blk = zl.at[zs[n], row, xs[j]]
            send(blk, blk, to_z[m], 0, zc[j][2])

    def y_block(j, n, rows=slice(None)):
        return yl.at[ys[n], k, rows, xs[j], pl.ds(0, depth[j])]

    def y_send(j):
        src = zl.at[z, :, xs[j], pl.ds(0, depth[j])]
        dst = y_block(j, 0)
        yc[j] = [send(src, dst, to_y[2], 1), send(src, dst, to_y[1], 1), arrival()]
        yp[j] = send(src, dst, partner, 2)
        own_copies.append(copy(src, dst))

    def y_forward(j):
        for n, row, m in ((1, 0, 2), (2, 1, 1)):
            await_tiles(yc[j][n - 1])
            blk = y_block(j, n, row)
            send(blk, blk, to_y[m], 1, yc[j][2])
            blk = y_block(j, n)
            send(blk, blk, partner, 2, yp[j])

    def y_finish(j):
        await_tiles(yc[j][2])
        blk = y_block(j, 3)
        send(blk, blk, partner, 2, yp[j])

    half = lax.rem(x, 2)
    red, last = {}, {}

    def lhs_of(q):
        rows = [
            jnp.concatenate(
                [zl[dz, i, dx, q] for dz in range(4) for dx in range(4)], axis=1
            )
            for i in range(2)
        ]
        return jnp.concatenate(rows, axis=0)

    def rhs_of(p, columns):
        rows = [
            jnp.concatenate(
                [ag[p, d // 4, d % 4 // 2, d % 2, c] for c in columns], axis=1
            )
            for d in range(16)
        ]
        return jnp.concatenate(rows, axis=0)

    def first_half(p, q):
        if q < 2:
            g[p, :, q * 512 : (q + 1) * 512] = jnp.dot(
                lhs_of(q), rhs_of(p, range(4)), preferred_element_type=F32
            ).astype(BF16)
        else:
            g[p, :, 1024:1280] = jnp.dot(
                lhs_of(2), rhs_of(p, (half, half + 2)), preferred_element_type=F32
            ).astype(BF16)

    def second_half(p, n):
        ay = zs[n]

        def tile_pair(ak, carry):
            rows = []
            for i in range(2):
                tiles = [yl[ay, ak, i, c, q] for q in range(2) for c in range(4)]
                tiles += [yl[ay, ak, i, half + 2 * c, 2] for c in range(2)]
                rows.append(jnp.concatenate(tiles, axis=1))
            right = jnp.concatenate(rows, axis=0)
            res = lax.dot_general(
                g[p],
                right,
                (((1,), (1,)), ((), ())),
                preferred_element_type=F32,
            ).astype(BF16)
            for i in range(2):
                for n in range(2):
                    ob[p, i, ay, 2 * ak + n] = res[
                        i * 128 : (i + 1) * 128, n * 128 : (n + 1) * 128
                    ]
            return carry

        lax.fori_loop(0, 2, tile_pair, 0)
        if p not in red:
            red[p] = [arrival(), arrival()]
        if n:
            send(ob.at[p, 0, ay], rz.at[p, z], to_z[n], 5, red[p][0])
        for m in (3, 1, 2):
            src = ob.at[p, 1, ay, xs[m]]
            send(src, rx.at[p, x, ay], to_x[m], 5, red[p][1])
        if not n:
            rz[p, z] = ob[p, 0, z]
            rx[p, x] = ob[p, 1, :, x]

    def total(ref, p):
        acc = ref[p, 0].astype(F32)
        for n in range(1, 4):
            acc = acc + ref[p, n].astype(F32)
        return acc.astype(BF16)

    def reduce_first(p):
        last[p] = [arrival(), arrival()]
        await_tiles(red[p][0])
        s0[p] = total(rz, p)
        for n in (3, 1, 2):
            send(s0.at[p, xs[n]], f0.at[p, x], to_x[n], 5, last[p][0])
        f0[p, x] = s0[p, x]
        await_tiles(red[p][1])
        s1[p] = total(rx, p)
        for n in (3, 1, 2):
            send(s1.at[p, zs[n]], f1.at[p, z], to_z[n], 5, last[p][1])
        f1[p, z] = s1[p, z]

    def reduce_last(p):
        for i, ref in enumerate((f0, f1)):
            await_tiles(last[p][i])
            tile = total(ref, p)
            if p:
                out[i, 0, (1, 3)[p - 1]] = tile
            if p < 2:
                fo[p, i] = tile

    z_send(0)
    y_send(0)
    a0.spread_second(0)
    a0.middle()
    a0.across()
    y_forward(0)
    z_forward(0)
    await_tiles(spread[1])
    z_send(1)
    y_send(1)
    await_tiles(spread[2])
    z_send(2)
    y_send(2)
    await_tiles(spread[3])
    z_send(3)
    a0.forward(0)
    form(1)
    a1.start()
    a1.spread_second(0)
    form(2)
    a2.start()
    y_send(3)
    a0.forward(1)
    a0.forward(2)
    y_forward(1)
    z_forward(1)
    a1.middle()
    a2.spread_second(0)
    a2.middle()
    y_forward(2)
    a0.forward(3)
    a1.across()
    a2.across()
    z_forward(2)
    a0.hand_near()
    y_finish(0)
    y_finish(1)
    a0.hand_far()
    z_forward(3)
    y_forward(3)
    y_finish(2)
    a1.forward(0)
    a1.forward(1)
    a1.forward(2)
    a1.forward(3)
    a1.hand_near()
    a2.forward(0)
    for j in range(4):
        await_tiles(zc[j][2])
    a0.done()
    first_half(0, 0)
    y_finish(3)
    a2.forward(1)
    a2.forward(2)
    first_half(0, 1)
    a1.hand_far()
    a2.forward(3)
    a2.hand_near()
    first_half(0, 2)
    for j in range(4):
        await_tiles(yp[j])
    for cp in own_copies:
        cp.wait()
    second_half(0, 3)
    second_half(0, 1)
    a2.hand_far()
    second_half(0, 2)
    second_half(0, 0)
    a1.done()
    for q in range(3):
        first_half(1, q)
    for n in (3, 1, 2, 0):
        second_half(1, n)
    reduce_first(0)
    a2.done()
    for q in range(3):
        first_half(2, q)
    reduce_last(0)
    back0 = exchange(lambda i: fo.at[0, i], lambda i: mo.at[0, i])
    second_half(2, 3)
    second_half(2, 1)
    reduce_first(1)
    second_half(2, 2)
    second_half(2, 0)
    reduce_last(1)
    back1 = exchange(lambda i: fo.at[1, i], lambda i: mo.at[1, i])
    exchange_wait(back0)
    for i in range(2):
        diff = fo[0, i].astype(F32) - mo[0, i].astype(F32).T
        out[i, 0, 0] = diff.astype(BF16)
    reduce_first(2)
    exchange_wait(back1)
    for i in range(2):
        out[i, 0, 2] = (-mo[1, i].astype(F32).T).astype(BF16)
    reduce_last(2)
    for n in range(SENDS):
        await_tiles([ssem.at[n], load[n]])


def body(amplitudes, cholesky, tile_mask):
    vec = cholesky[:, 0]
    vmem = pl.BlockSpec(memory_space=pltpu.VMEM)
    tile = (128, 128)
    return pl.pallas_call(
        kernel,
        out_shape=jax.ShapeDtypeStruct((2, 1, 4) + tile, BF16),
        in_specs=[pl.BlockSpec(memory_space=pltpu.SMEM), vmem, vmem],
        out_specs=vmem,
        scratch_shapes=[
            pltpu.VMEM((2, 3) + tile, BF16),
            pltpu.VMEM((4, 2, 4, 3) + tile, BF16),
            pltpu.VMEM((4, 2, 2, 4, 3) + tile, BF16),
            pltpu.VMEM((3, 4, 2, 2, 4) + tile, BF16),
            pltpu.VMEM((2, 2) + tile, BF16),
            pltpu.VMEM((3, 256, 1280), BF16),
            pltpu.VMEM((3, 2, 4, 4) + tile, BF16),
            pltpu.VMEM((3, 4, 4) + tile, BF16),
            pltpu.VMEM((3, 4, 4) + tile, BF16),
            pltpu.VMEM((3, 4) + tile, BF16),
            pltpu.VMEM((3, 4) + tile, BF16),
            pltpu.VMEM((3, 4) + tile, BF16),
            pltpu.VMEM((3, 4) + tile, BF16),
            pltpu.VMEM((2, 2) + tile, BF16),
            pltpu.VMEM((2, 2) + tile, BF16),
            pltpu.VMEM((256,) + tile, BF16),
            pltpu.SemaphoreType.DMA((SENDS,)),
            pltpu.SemaphoreType.DMA((RECVS,)),
            pltpu.SemaphoreType.DMA((LOCALS,)),
            pltpu.SemaphoreType.DMA((24,)),
        ],
        compiler_params=pltpu.CompilerParams(
            collective_id=0, has_side_effects=True, vmem_limit_bytes=56 * 1024 * 1024
        ),
    )(tile_mask.T, vec, amplitudes)


def solution(mesh):
    in_specs = (
        P("row", "col", None, None, None),
        P("row", "col", None, None, None),
        P("row", "col"),
    )
    out_specs = P("row", "col", None, None, None)
    return jax.shard_map(
        body, mesh=mesh, in_specs=in_specs, out_specs=out_specs, check_vma=False
    )
```

time: 315 us -> 86.7 us (0.28)
  waiting for transfers between devices: 164 us -> 0 us
  Pallas kernels: 0 us -> 83.4 us
  blocking collectives: 76.8 us -> 0 us
  matrix products: 19.9 us -> 0 us
  starting transfers between devices: 16.7 us -> 0 us
  between operations: 14 us -> 0.01 us
  local copies, waits for them, and re-layouts: 12.7 us -> 1.67 us
  other arithmetic: 6.55 us -> 0 us
    all_gather x3 -> x0, waiting for transfers between devices: 127 us -> none  [the longest x1 64.7 us: body(): spread = lax.all_gather(cholesky, 'col', axis=1, tiled=True)]
    pallas_call x0 -> x1, Pallas kernels: none -> 83.4 us  [body(): pl.pallas_call(kernel, out_shape=jax.ShapeDtypeStruct((2, 1, 4) + tile, B...]
    unnamed x1 -> x0, blocking collectives: 55 us -> none
    ppermute x10 -> x0, waiting for transfers between devices: 34.8 us -> none  [from_partner(): return lax.ppermute(value, axis, pairs)]
    all_gather x1 -> x0, blocking collectives: 21.9 us -> none  [body(): mask_block = lax.all_gather(tile_mask, 'col', axis=1, tiled=True)]
    dot_general x2 -> x0, matrix products: 19.9 us -> none  [the longest x1 10.9 us: body(): jnp.einsum('caqux,cpuqy->apxy', spread, halves, preferred_element_type=jn...]
    ppermute x10 -> x0, starting transfers between devices: 16.7 us -> none  [from_partner(): return lax.ppermute(value, axis, pairs)]
    all_gather x2 -> x0, local copies, waits for them, and re-layouts: 7.87 us -> none  [the longest x1 7.8 us: body(): column = lax.all_gather(cholesky, 'row', axis=0, tiled=True)]
  transfers between devices with their start and end apart: 13 -> 0, of which waited for: 13 -> 0; matrix products, arithmetic and copies ran while one was open for 8% -> 0% of each run, Pallas kernels for 0% -> 0%
where the time goes in v2:
time: 86.7 us; the launch traced here: 85 us
  Pallas kernels  83.4 us (96%)
  local copies, waits for them, and re-layouts  1.67 us (2%)
    pallas_call x1, Pallas kernels, body(): pl.pallas_call(kernel, out_shape=jax.ShapeDtypeStruct((2, 1, 4) + tile, B...  83.4 us

profile of v2, /device:TPU:24, one launch (start us, length us, event | category | flops | bytes accessed | tf_op | source)
XLA Modules:
  0.0 85.0 jit_solution(11971959453042849465)
XLA Ops:
  0.0 83.4 %shard_map.37 = bf16[2,1,4,128,128]{4,3,2,1,0:T(8,128)(2,1)} custom-call(s32[1,2]{1,0:T(1,128)} %bitcast.3, bf16[2,10,128,128]{3,2,1,0:T(8,128)(2,1)} %bitcast.2, bf16[2,1,4,128,128]{4,3,2,1,0:T(8,128)(2,1)} %t_in.1), custom_call_target="tpu_custom_call" | custom-call | tf_op jit(solution)/shard_map/pallas_call | solution.py:458
  83.4 1.7 %copy.5 = bf16[2,1,4,128,128]{4,3,2,1,0:T(8,128)(2,1)} copy(bf16[2,1,4,128,128]{4,3,2,1,0:T(8,128)(2,1)} %shard_map.37) | data formatting | bytes 524288

commit v3 on v2

--- a/solution.py
+++ b/solution.py
@@ -17,7 +17,7 @@
 
 def kernel(
     mask, lin, t_in, out, t, zl, yl, ag, mt, g, ob, rz, rx, s0, s1, f0, f1, fo, mo,
-    size, ssem, rsem, lsem, xsem,
+    qz, qx, cz, cx, size, ssem, rsem, lsem, xsem,
 ):
     r = lax.axis_index("row")
     col = lax.axis_index("col")
@@ -200,10 +200,11 @@
     a0, a1, a2 = (Gather(p, True) for p in range(3))
 
     a0.start()
-    swaps = [
-        exchange(lambda i, q=q: t.at[i, q], lambda i, q=q: mt.at[q - 1, i])
-        for q in (1, 2)
-    ]
+    def swap(q):
+        swaps.append(exchange(lambda i: t.at[i, q], lambda i: mt.at[q - 1, i]))
+
+    swaps = []
+    swap(1)
 
     def form(p):
         own, other = ((0, 0), (2, 1))[p - 1]
@@ -259,7 +260,7 @@
         send(blk, blk, partner, 2, yp[j])
 
     half = lax.rem(x, 2)
-    red, last = {}, {}
+    red, relay, last = {}, {}, {}
 
     def lhs_of(q):
         rows = [
@@ -315,18 +316,45 @@
         lax.fori_loop(0, 2, tile_pair, 0)
         if p not in red:
             red[p] = [arrival(), arrival()]
-        if n:
-            send(ob.at[p, 0, ay], rz.at[p, z], to_z[n], 5, red[p][0])
-        for m in (3, 1, 2):
-            src = ob.at[p, 1, ay, xs[m]]
-            send(src, rx.at[p, x, ay], to_x[m], 5, red[p][1])
-        if not n:
-            rz[p, z] = ob[p, 0, z]
-            rx[p, x] = ob[p, 1, :, x]
+            relay[p] = [arrival(), arrival()]
+        lo, hi = pl.ds(0, 2), pl.ds(2, 2)
+        row = ob.at[p, 0, ay]
+        if n == 3:
+            send(row.at[lo], qz.at[p, lo], to_z[2], 5, relay[p][0])
+            send(row.at[hi], qz.at[p, hi], to_z[1], 5, relay[p][0])
+        elif n == 2:
+            send(row.at[hi], rz.at[p, 1, hi], to_z[2], 5, red[p][0])
+        elif n == 1:
+            send(row.at[lo], rz.at[p, 2, lo], to_z[1], 5, red[p][0])
+        else:
+            rz[p, 0] = ob[p, 0, z]
+        up = n in (3, 1)
+        tile = ob.at[p, 1, ay]
+        send(tile.at[xs[3]], qx.at[p, ay], to_x[2 if up else 1], 5, relay[p][1])
+        if up:
+            send(tile.at[xs[1]], rx.at[p, 2, ay], to_x[1], 5, red[p][1])
+        else:
+            send(tile.at[xs[2]], rx.at[p, 1, ay], to_x[2], 5, red[p][1])
+        rx[p, 0, ay] = ob[p, 1, ay, x]
+
+    def reduce_relayed(p):
+        await_tiles(relay[p][0])
+        for n, m, part in ((2, 1, slice(0, 2)), (1, 2, slice(2, 4))):
+            both = ob[p, 0, zs[n], part].astype(F32) + qz[p, part].astype(F32)
+            cz[p, part] = both.astype(BF16)
+            part = pl.ds(part.start, 2)
+            send(cz.at[p, part], rz.at[p, m, part], to_z[n], 5, red[p][0])
+        await_tiles(relay[p][1])
+        for n in (3, 1, 2, 0):
+            b, m = (2, 1) if n in (3, 1) else (1, 2)
+            at = zs[n]
+            both = ob[p, 1, at, xs[b]].astype(F32) + qx[p, at].astype(F32)
+            cx[p, at] = both.astype(BF16)
+            send(cx.at[p, at], rx.at[p, m, at], to_x[b], 5, red[p][1])
 
     def total(ref, p):
         acc = ref[p, 0].astype(F32)
-        for n in range(1, 4):
+        for n in range(1, ref.shape[1]):
             acc = acc + ref[p, n].astype(F32)
         return acc.astype(BF16)
 
@@ -356,6 +384,7 @@
     y_send(0)
     a0.spread_second(0)
     a0.middle()
+    swap(2)
     a0.across()
     y_forward(0)
     z_forward(0)
@@ -423,19 +452,23 @@
     a1.done()
     for q in range(3):
         first_half(1, q)
+    reduce_relayed(0)
     for n in (3, 1, 2, 0):
         second_half(1, n)
     reduce_first(0)
     a2.done()
-    for q in range(3):
-        first_half(2, q)
+    first_half(2, 0)
+    first_half(2, 1)
+    reduce_relayed(1)
+    first_half(2, 2)
     reduce_last(0)
     back0 = exchange(lambda i: fo.at[0, i], lambda i: mo.at[0, i])
     second_half(2, 3)
     second_half(2, 1)
-    reduce_first(1)
     second_half(2, 2)
     second_half(2, 0)
+    reduce_first(1)
+    reduce_relayed(2)
     reduce_last(1)
     back1 = exchange(lambda i: fo.at[1, i], lambda i: mo.at[1, i])
     exchange_wait(back0)
@@ -468,14 +501,18 @@
             pltpu.VMEM((2, 2) + tile, BF16),
             pltpu.VMEM((3, 256, 1280), BF16),
             pltpu.VMEM((3, 2, 4, 4) + tile, BF16),
-            pltpu.VMEM((3, 4, 4) + tile, BF16),
-            pltpu.VMEM((3, 4, 4) + tile, BF16),
+            pltpu.VMEM((3, 3, 4) + tile, BF16),
+            pltpu.VMEM((3, 3, 4) + tile, BF16),
             pltpu.VMEM((3, 4) + tile, BF16),
             pltpu.VMEM((3, 4) + tile, BF16),
             pltpu.VMEM((3, 4) + tile, BF16),
             pltpu.VMEM((3, 4) + tile, BF16),
             pltpu.VMEM((2, 2) + tile, BF16),
             pltpu.VMEM((2, 2) + tile, BF16),
+            pltpu.VMEM((3, 4) + tile, BF16),
+            pltpu.VMEM((3, 4) + tile, BF16),
+            pltpu.VMEM((3, 4) + tile, BF16),
+            pltpu.VMEM((3, 4) + tile, BF16),
             pltpu.VMEM((256,) + tile, BF16),
             pltpu.SemaphoreType.DMA((SENDS,)),
             pltpu.SemaphoreType.DMA((RECVS,)),

time: 86.7 us -> 84.1 us (0.970)
  Pallas kernels: 83.4 us -> 81.4 us
    pallas_call x1, Pallas kernels: 83.4 us -> 81.4 us  [body(): pl.pallas_call(kernel, out_shape=jax.ShapeDtypeStruct((2, 1, 4) + tile, B...]
where the time goes in v3:
time: 84.1 us; the launch traced here: 83.1 us
  Pallas kernels  81.4 us (97%)
  local copies, waits for them, and re-layouts  1.67 us (2%)
    pallas_call x1, Pallas kernels, body(): pl.pallas_call(kernel, out_shape=jax.ShapeDtypeStruct((2, 1, 4) + tile, B...  81.4 us

profile of v3, /device:TPU:24, one launch (start us, length us, event | category | flops | bytes accessed | tf_op | source)
XLA Modules:
  0.0 83.1 jit_solution(2747394480511046420)
XLA Ops:
  0.0 81.4 %shard_map.37 = bf16[2,1,4,128,128]{4,3,2,1,0:T(8,128)(2,1)} custom-call(s32[1,2]{1,0:T(1,128)} %bitcast.3, bf16[2,10,128,128]{3,2,1,0:T(8,128)(2,1)} %bitcast.2, bf16[2,1,4,128,128]{4,3,2,1,0:T(8,128)(2,1)} %t_in.1), custom_call_target="tpu_custom_call" | custom-call | tf_op jit(solution)/shard_map/pallas_call | solution.py:491
  81.4 1.7 %copy.5 = bf16[2,1,4,128,128]{4,3,2,1,0:T(8,128)(2,1)} copy(bf16[2,1,4,128,128]{4,3,2,1,0:T(8,128)(2,1)} %shard_map.37) | data formatting | bytes 524288

commit v4 on v3

--- a/solution.py
+++ b/solution.py
@@ -11,8 +11,8 @@
 BF16 = jnp.bfloat16
 F32 = jnp.float32
 SENDS = 6
-RECVS = 110
-LOCALS = 16
+RECVS = 88
+LOCALS = 6
 
 
 def kernel(
@@ -471,11 +471,11 @@
     reduce_relayed(2)
     reduce_last(1)
     back1 = exchange(lambda i: fo.at[1, i], lambda i: mo.at[1, i])
+    reduce_first(2)
     exchange_wait(back0)
     for i in range(2):
         diff = fo[0, i].astype(F32) - mo[0, i].astype(F32).T
         out[i, 0, 0] = diff.astype(BF16)
-    reduce_first(2)
     exchange_wait(back1)
     for i in range(2):
         out[i, 0, 2] = (-mo[1, i].astype(F32).T).astype(BF16)

time: 84.1 us -> 83.8 us (level)
  no operation moved by 1% of the time
where the time goes in v4:
time: 83.8 us; the launch traced here: 82.8 us
  Pallas kernels  81.1 us (97%)
  local copies, waits for them, and re-layouts  1.67 us (2%)
    pallas_call x1, Pallas kernels, body(): pl.pallas_call(kernel, out_shape=jax.ShapeDtypeStruct((2, 1, 4) + tile, B...  81.1 us

profile of v4, /device:TPU:24, one launch (start us, length us, event | category | flops | bytes accessed | tf_op | source)
XLA Modules:
  0.0 82.8 jit_solution(8121738149877987366)
XLA Ops:
  0.0 81.1 %shard_map.37 = bf16[2,1,4,128,128]{4,3,2,1,0:T(8,128)(2,1)} custom-call(s32[1,2]{1,0:T(1,128)} %bitcast.3, bf16[2,10,128,128]{3,2,1,0:T(8,128)(2,1)} %bitcast.2, bf16[2,1,4,128,128]{4,3,2,1,0:T(8,128)(2,1)} %t_in.1), custom_call_target="tpu_custom_call" | custom-call | tf_op jit(solution)/shard_map/pallas_call | solution.py:491
  81.1 1.7 %copy.5 = bf16[2,1,4,128,128]{4,3,2,1,0:T(8,128)(2,1)} copy(bf16[2,1,4,128,128]{4,3,2,1,0:T(8,128)(2,1)} %shard_map.37) | data formatting | bytes 524288
